TPU v7x, 256 devices: a whole 4x4x8 slice. The times are simulated.
256 devices in a mesh: gen: 8 (over z_lo, core), user: 16 (over x, y), cand: 2 (over z_hi).
Axes of the slice: x: 4, y: 4, z: 8 (z_hi: 2, z_lo: 4; z = z_hi * 4 + z_lo), core: 2. Of those that a mesh axis runs over, the one named last changes fastest.
Arguments:
- states: bfloat16 [16384, 4096], P(('user', 'cand')), may hold values from -6 to 6
- norm_gain: float32 [4096], replicated, may hold values from 0.1 to 1.9
- gate_weight: bfloat16 [4096, 7168], P('user', 'gen'), may hold values from -0.09375 to 0.09375
- up_weight: bfloat16 [4096, 7168], P('user', 'gen'), may hold values from -0.09375 to 0.09375
- down_weight: bfloat16 [7168, 4096], P('gen', 'user'), may hold values from -0.0625 to 0.0625
- proj_weight: bfloat16 [4096, 1024], P('gen'), may hold values from -0.09375 to 0.09375
- private_rows: bfloat16 [32768, 1024], P(('gen', 'user')), may hold values from -6 to 6
- enc_weight: bfloat16 [1024, 1024], replicated, may hold values from -0.1875 to 0.1875
- user_ids: int32 [32768], P(('gen', 'user')), may hold values from 0 to 31
Outputs:
- votes: float32 [16, 2, 128], P(None, 'cand')
Inputs may be any that keep to these rules, and one draw needn't show every extreme that they name: `user_ids`: a user is a pair of a block of 256 rows and a slot; no user has rows in two blocks.
All inputs are finite; a program needn't handle non-finite values.
Results may differ from a plain program's by a relative error of at most 0.0025.
Values may be sent and summed in bfloat16 or wider, within the bound.
No kernel may reach another device: no remote copies, remote signals or barrier semaphores. Data moves between devices by JAX's collectives and lax.ppermute only.
A program may use at most 128 MiB of HBM per device.

v0:
```python
import jax
import jax.numpy as jnp
from jax import lax
from jax.sharding import PartitionSpec as P

STEPS = 4
CAP = 8
USERS_DEV = 32


def unit_rows(matrix):
    return (matrix * lax.rsqrt(jnp.sum(matrix * matrix, axis=1, keepdims=True) + 1e-06)).astype(
        jnp.bfloat16
    )


def project_in(inputs, gate_part, up_part):

    def add_rows(piece):
        return jnp.dot(inputs, piece, preferred_element_type=jnp.float32)

    gate = add_rows(lax.all_gather(gate_part, "user", axis=0, tiled=True))
    up_proj = add_rows(lax.all_gather(up_part, "user", axis=0, tiled=True))
    return (gate, up_proj)


def shards(
    states,
    norm_gain,
    gate_weight,
    up_weight,
    down_weight,
    proj_weight,
    private_rows,
    enc_weight,
    user_ids,
):
    tok_rows, width_model = states.shape
    groups = tok_rows // STEPS
    values = states.astype(jnp.float32)
    normed = (
        values * lax.rsqrt(jnp.mean(values * values, axis=1, keepdims=True) + 1e-05) * norm_gain
    ).astype(jnp.bfloat16)
    gate_part, up_part, down_part = (gate_weight, up_weight, down_weight)
    gate, up_proj = project_in(normed, gate_part, up_part)
    hidden = (jax.nn.silu(gate) * up_proj).astype(jnp.bfloat16)
    mixed = jnp.dot(
        hidden,
        lax.all_gather(down_part, "user", axis=1, tiled=True),
        preferred_element_type=jnp.float32,
    )
    pooled_mlp = jnp.sum(mixed.reshape(-1, STEPS, width_model), axis=1)
    pooled_mlp = lax.psum_scatter(pooled_mlp, "gen", scatter_dimension=1, tiled=True)
    slab_width = pooled_mlp.shape[1]
    own_cols = lax.dynamic_slice_in_dim(values, lax.axis_index("gen") * slab_width, slab_width, 1)
    pooled_in = jnp.sum(own_cols.reshape(groups, STEPS, slab_width), axis=1)
    pooled = ((pooled_in + pooled_mlp) / STEPS).astype(jnp.bfloat16)
    partial_emb = jnp.dot(pooled, proj_weight, preferred_element_type=jnp.float32)
    embedding = lax.psum(partial_emb, "gen")
    candidate = unit_rows(embedding)
    every_cand = lax.all_gather(candidate, "user", axis=0, tiled=True)
    encoded = unit_rows(jnp.dot(private_rows, enc_weight, preferred_element_type=jnp.float32))
    scores = lax.dot_general(
        encoded, every_cand, (((1,), (1,)), ((), ())), preferred_element_type=jnp.float32
    )
    kernel = jnp.exp(scores * 60.0)
    totals = lax.psum(jnp.sum(kernel, axis=1), "cand")
    member = (user_ids[:, None] == jnp.arange(USERS_DEV, dtype=jnp.int32)[None, :]).astype(
        jnp.float32
    )
    counts = jnp.sum(member, axis=0)
    limit = jnp.minimum(1.0, CAP / jnp.maximum(counts, 1.0))
    row_cap = jnp.dot(member, limit, precision=lax.Precision.HIGHEST)
    row_total = private_rows.shape[0] * lax.axis_size("gen") * lax.axis_size("user")
    cand_total = every_cand.shape[0] * lax.axis_size("cand")
    weight_rows = row_cap / totals * (cand_total / row_total)
    partial_votes = jnp.dot(weight_rows, kernel, precision=lax.Precision.HIGHEST)
    votes = lax.psum(partial_votes, ("gen", "user"))
    return votes.reshape(lax.axis_size("user"), 1, groups)


def solution(mesh):
    return jax.shard_map(
        shards,
        mesh=mesh,
        in_specs=(
            P(("user", "cand"), None),
            P(),
            P("user", "gen"),
            P("user", "gen"),
            P("gen", "user"),
            P("gen", None),
            P(("gen", "user"), None),
            P(),
            P(("gen", "user")),
        ),
        out_specs=P(None, "cand", None),
        check_vma=False,
    )
```

profile of v0, /device:TPU:0, one launch (start us, length us, event | category | flops | bytes accessed | tf_op | source)
XLA Modules:
  0.0 810.1 jit_solution(10870717847516051505)
XLA Ops:
  6.5 0.7 all-gather.5.cloned.1.call-update
  7.3 0.0 all-gather.7.cloned.1.call-start
  7.3 0.7 all-gather.7.cloned.1.call-update
  8.1 0.7 all-gather.9.cloned.1.call-update
  8.7 0.0 reduce-scatter.2.cloned.1.call-start
  8.8 3.1 multiply_reduce_fusion
  11.9 70.3 %all-gather.5.cloned.1.call-done = bf16[4096,896]{1,0:T(8,128)(2,1)} async-done(((bf16[256,896]{1,0:T(8,128)(2,1)}), bf16[4096,896]{1,0:T(8,128)(2,1)}) %all-gather.5.cloned.1.call-update) | async-done | bytes 7340048 | tf_op jit(solution)/shard_map/all_gather | solution.py:22
  82.2 10.1 %fusion.1 = f32[512,896]{1,0:T(8,128)} fusion(bf16[4096,896]{1,0:T(8,128)(2,1)} %all-gather.5.cloned.1.call-done, f32[4096]{0:T(1024)S(1)} %copy-done.1, f32[512]{0:T(512)S(1)} %add_rsqrt_fusion, bf16[512,4096]{1,0:T(8,128)(2,1)} %param.9), kind=kOutput, calls=%fused_computation.5 | convolution fusion | flops 3766484992 | bytes 13387776 | tf_op jit(solution)/shard_map/dot_general | solution.py:20
  92.3 63.2 %all-gather.7.cloned.1.call-done = bf16[4096,896]{1,0:T(8,128)(2,1)} async-done(((bf16[256,896]{1,0:T(8,128)(2,1)}), bf16[4096,896]{1,0:T(8,128)(2,1)}) %all-gather.7.cloned.1.call-update) | async-done | bytes 7340048 | tf_op jit(solution)/shard_map/all_gather | solution.py:23
  155.6 79.3 %all-gather.9.cloned.1.call-done = bf16[896,4096]{1,0:T(8,128)(2,1)} async-done(((bf16[896,256]{1,0:T(8,128)(2,1)}), bf16[896,4096]{1,0:T(8,128)(2,1)}) %all-gather.9.cloned.1.call-update) | async-done | bytes 7340048 | tf_op jit(solution)/shard_map/all_gather | solution.py:49
  234.8 17.4 %fusion.2 = f32[512,4096]{1,0:T(8,128)} fusion(bf16[896,4096]{1,0:T(8,128)(2,1)} %all-gather.9.cloned.1.call-done, f32[512,896]{1,0:T(8,128)} %fusion.1, bf16[4096,896]{1,0:T(8,128)(2,1)} %all-gather.7.cloned.1.call-done, f32[4096]{0:T(1024)S(1)} %copy-done.1, f32[512]{0:T(512)S(1)} %add_rsqrt_fusion, bf16[512,4096]{1,0:T(8,128)(2,1)} %param.9), kind=kOutput, calls=%fused_computation.9 | convolution fusion | flops 7527333888 | bytes 29116416 | tf_op jit(solution)/shard_map/dot_general | solution.py:47
  252.2 9.8 %reshape.32 = f32[128,4,4096]{2,1,0:T(4,128)} reshape(f32[512,4096]{1,0:T(8,128)} %fusion.2) | data formatting | bytes 16777216 | tf_op jit(solution)/shard_map/reshape | solution.py:52
  262.0 10.0 %reduce_sum.67 = f32[128,4096]{1,0:T(8,128)} reduce(f32[128,4,4096]{2,1,0:T(4,128)} %reshape.32, f32[]{:T(128)} %constant.15.clone.1), dimensions={1}, to_apply=%region_4.5 | reduce | flops 1572864 | bytes 10485764 | tf_op jit(solution)/shard_map/reduce_sum | solution.py:52
  272.1 0.0 all-reduce.2.cloned.1.call-start
  272.1 6.5 convert_element_type.23
  278.6 1.3 constant_dynamic-slice_fusion
  279.9 1.3 reshape.31
  281.2 1.8 reduce_sum.65
  283.1 29.9 %reduce-scatter.2.cloned.1.call-done = f32[128,512]{1,0:T(8,128)} async-done(((f32[128,4096]{1,0:T(8,128)}), f32[128,512]{1,0:T(8,128)}) %reduce-scatter.2.cloned.1.call-update) | async-done | bytes 262160 | tf_op jit(solution)/shard_map/reduce_scatter | solution.py:53
  313.0 2.4 fusion.4
  315.4 0.3 all-gather.11.cloned.1.call-start
  315.7 70.7 %all-reduce.2.cloned.1.call-done = f32[128,1024]{1,0:T(8,128)} async-done(((f32[128,1024]{1,0:T(8,128)}), f32[128,1024]{1,0:T(8,128)}) %all-reduce.2.cloned.1.call-update) | async-done | bytes 524304 | tf_op jit(solution)/shard_map/psum | solution.py:59
  386.3 1.2 multiply_reduce_fusion.2
  387.5 1.8 multiply_convert_fusion.8
  389.4 0.1 convert_reduce_fusion
  389.5 1.8 multiply_reduce_fusion.1
  391.3 0.1 fusion.6
  391.5 53.5 %all-gather.11.cloned.1.call-done = bf16[2048,1024]{1,0:T(8,128)(2,1)} async-done(((bf16[128,1024]{1,0:T(8,128)(2,1)}), bf16[2048,1024]{1,0:T(8,128)(2,1)}) %all-gather.11.cloned.1.call-update) | async-done | bytes 4194320 | tf_op jit(solution)/shard_map/all_gather | solution.py:61
  445.0 4.9 fusion.16
  449.8 8.8 %psum.22 = f32[256]{0:T(256)S(1)} all-reduce(f32[256]{0:T(256)S(1)} %get-tuple-element.7), channel_id=1, replica_groups=mesh['gen'=8,'user'=16,'cand'=2] {'cand'}, use_global_device_ids=true, to_apply=%region_9.10 | all-reduce | flops 256 | bytes 2048 | tf_op jit(solution)/shard_map/psum | solution.py:67
  458.6 2.7 convolution_bitcast_fusion
  461.3 341.9 %psum.23 = f32[16,1,128]{2,1,0:T(1,128)} all-reduce(f32[16,1,128]{2,1,0:T(1,128)S(1)} %convolution_bitcast_fusion), channel_id=1, replica_groups=mesh['gen'=8,'user'=16,'cand'=2] {'gen','user'}, use_global_device_ids=true, to_apply=%region_10.11 | all-reduce | flops 2048 | bytes 16384 | tf_op jit(solution)/shard_map/psum | solution.py:78
  (15 shorter events, 0.1 us)
Async XLA Ops:
  6.5 383.0 %copy-start = (bf16[1024,1024]{1,0:T(8,128)(2,1)S(1)}, bf16[1024,1024]{1,0:T(8,128)(2,1)}, u32[]{:S(2)}) copy-start(bf16[1024,1024]{1,0:T(8,128)(2,1)} %param.16) | copy-start | bytes 6291460
  6.5 75.7 %copy-start.1 = (f32[4096]{0:T(1024)S(1)}, f32[4096]{0:T(1024)}, u32[]{:S(2)}) copy-start(f32[4096]{0:T(1024)} %param.10) | copy-start | bytes 49156
  6.5 75.7 %all-gather.5.cloned.1.call-start = ((), (), s32[]{:S(2)}) async-start(), calls=%async_computation.1 | async-start | bytes 7798784 | tf_op jit(solution)/shard_map/all_gather | solution.py:22
  7.3 148.3 %all-gather.7.cloned.1.call-start = ((), (), s32[]{:S(2)}) async-start(), calls=%async_computation.2 | async-start | bytes 7798784 | tf_op jit(solution)/shard_map/all_gather | solution.py:23
  8.0 226.8 %all-gather.9.cloned.1.call-start = ((), (), s32[]{:S(2)}) async-start(), calls=%async_computation.3 | async-start | bytes 7798784 | tf_op jit(solution)/shard_map/all_gather | solution.py:49
  8.7 304.2 %reduce-scatter.2.cloned.1.call-start = ((), (), s32[]{:S(2)}) async-start(), calls=%async_computation.4 | async-start | bytes 2359296 | tf_op jit(solution)/shard_map/reduce_scatter | solution.py:53
  272.1 114.3 %all-reduce.2.cloned.1.call-start = ((), (), s32[]{:S(2)}) async-start(), calls=%async_computation.5 | async-start | bytes 1048576 | tf_op jit(solution)/shard_map/psum | solution.py:59
  279.9 109.5 %copy-start.2 = (s32[256]{0:T(256)S(1)}, s32[256]{0:T(256)}, u32[]{:S(2)}) copy-start(s32[256]{0:T(256)} %param.17) | copy-start | bytes 3076
  315.4 129.5 %all-gather.11.cloned.1.call-start = ((), (), s32[]{:S(2)}) async-start(), calls=%async_computation.6 | async-start | bytes 4456448 | tf_op jit(solution)/shard_map/all_gather | solution.py:61
Sparse Core Ops, SparseCore 0:
  9.8 72.3 all-gather.4
  84.7 70.8 all-gather.6
  158.0 76.7 all-gather.8
  272.2 40.7 reduce-scatter.1
  315.5 70.7 all-reduce.1
  389.5 55.4 all-gather.10
where the time goes:
time: 811 us; the launch traced here: 810 us
  waiting for transfers between devices  369 us (45%)
  blocking collectives  351 us (43%)
  matrix products  39.5 us (5%)
  other arithmetic  24.6 us (3%)
  between operations  13.5 us (2%)
  local copies, waits for them, and re-layouts  12.4 us (2%)
    psum x1, blocking collectives, shards(): votes = lax.psum(partial_votes, ('gen', 'user'))  342 us
    all_gather x1, waiting for transfers between devices, shards(): lax.all_gather(down_part, 'user', axis=1, tiled=True)  79.3 us
    psum x1, waiting for transfers between devices, shards(): embedding = lax.psum(partial_emb, 'gen')  70.7 us
    all_gather x1, waiting for transfers between devices, project_in(): gate = add_rows(lax.all_gather(gate_part, 'user', axis=0, tiled=True))  70.3 us
    all_gather x1, waiting for transfers between devices, project_in(): up_proj = add_rows(lax.all_gather(up_part, 'user', axis=0, tiled=True))  63.2 us
    all_gather x1, waiting for transfers between devices, shards(): every_cand = lax.all_gather(candidate, 'user', axis=0, tiled=True)  53.5 us
    reduce_scatter x1, waiting for transfers between devices, shards(): lax.psum_scatter(pooled_mlp, 'gen', scatter_dimension=1, tiled=True)  29.9 us
    dot_general x1, matrix products, shards(): jnp.dot(hidden, lax.all_gather(down_part, 'user', axis=1, tiled=True), pr...  17.4 us
  transfers between devices with their start and end apart: 6, of which 6 were waited for; matrix products, arithmetic and copies ran while one was open for 3% of the time, Pallas kernels for 0%

commit v1 on v0

--- a/solution.py
+++ b/solution.py
@@ -75,7 +75,7 @@
     cand_total = every_cand.shape[0] * lax.axis_size("cand")
     weight_rows = row_cap / totals * (cand_total / row_total)
     partial_votes = jnp.dot(weight_rows, kernel, precision=lax.Precision.HIGHEST)
-    votes = lax.psum(partial_votes, ("gen", "user"))
+    votes = lax.all_gather(partial_votes, axis_name=("gen", "user")).sum(axis=0)
     return votes.reshape(lax.axis_size("user"), 1, groups)
 
 

time: 811 us -> 779 us (0.961)
  blocking collectives: 351 us -> 8.82 us
  waiting for transfers between devices: 369 us -> 673 us
    psum x1 -> x0, blocking collectives: 342 us -> none  [shards(): votes = lax.psum(partial_votes, ('gen', 'user'))]
    all_gather x0 -> x1, waiting for transfers between devices: none -> 304 us  [shards(): votes = lax.all_gather(partial_votes, axis_name=('gen', 'user')).sum(axis=0)]
  transfers between devices with their start and end apart: 6 -> 7, of which waited for: 6 -> 7; matrix products, arithmetic and copies ran while one was open for 3% -> 3% of each run, Pallas kernels for 0% -> 0%
where the time goes in v1:
time: 779 us; the launch traced here: 775 us
  waiting for transfers between devices  673 us (86%)
  matrix products  40.1 us (5%)
  other arithmetic  25.3 us (3%)
  local copies, waits for them, and re-layouts  13.8 us (2%)
  between operations  13.5 us (2%)
  blocking collectives  8.82 us (1%)
    all_gather x1, waiting for transfers between devices, shards(): votes = lax.all_gather(partial_votes, axis_name=('gen', 'user')).sum(axis=0)  304 us
    all_gather x1, waiting for transfers between devices, shards(): lax.all_gather(down_part, 'user', axis=1, tiled=True)  79.3 us
    psum x1, waiting for transfers between devices, shards(): embedding = lax.psum(partial_emb, 'gen')  70.9 us
    all_gather x1, waiting for transfers between devices, project_in(): gate = add_rows(lax.all_gather(gate_part, 'user', axis=0, tiled=True))  70.3 us
    all_gather x1, waiting for transfers between devices, project_in(): up_proj = add_rows(lax.all_gather(up_part, 'user', axis=0, tiled=True))  63.2 us
    all_gather x1, waiting for transfers between devices, shards(): every_cand = lax.all_gather(candidate, 'user', axis=0, tiled=True)  53.2 us
    reduce_scatter x1, waiting for transfers between devices, shards(): lax.psum_scatter(pooled_mlp, 'gen', scatter_dimension=1, tiled=True)  29.9 us
    dot_general x1, matrix products, shards(): jnp.dot(hidden, lax.all_gather(down_part, 'user', axis=1, tiled=True), pr...  17.4 us
  transfers between devices with their start and end apart: 7, of which 7 were waited for; matrix products, arithmetic and copies ran while one was open for 3% of the time, Pallas kernels for 0%

profile of v1, /device:TPU:0, one launch (start us, length us, event | category | flops | bytes accessed | tf_op | source)
XLA Modules:
  0.0 774.5 jit_solution(4845903373011978420)
XLA Ops:
  6.5 0.7 all-gather.7.cloned.1.call-update
  7.3 0.7 all-gather.9.cloned.1.call-update
  8.1 0.7 all-gather.11.cloned.1.call-update
  8.8 3.1 multiply_reduce_fusion
  11.9 70.3 %all-gather.7.cloned.1.call-done = bf16[4096,896]{1,0:T(8,128)(2,1)} async-done(((bf16[256,896]{1,0:T(8,128)(2,1)}), bf16[4096,896]{1,0:T(8,128)(2,1)}) %all-gather.7.cloned.1.call-update) | async-done | bytes 7340048 | tf_op jit(solution)/shard_map/all_gather | solution.py:22
  82.2 10.1 %fusion.1 = f32[512,896]{1,0:T(8,128)} fusion(bf16[4096,896]{1,0:T(8,128)(2,1)} %all-gather.7.cloned.1.call-done, f32[4096]{0:T(1024)S(1)} %copy-done.1, f32[512]{0:T(512)S(1)} %add_rsqrt_fusion, bf16[512,4096]{1,0:T(8,128)(2,1)} %param.9), kind=kOutput, calls=%fused_computation.5 | convolution fusion | flops 3766484992 | bytes 13387776 | tf_op jit(solution)/shard_map/dot_general | solution.py:20
  92.3 63.2 %all-gather.9.cloned.1.call-done = bf16[4096,896]{1,0:T(8,128)(2,1)} async-done(((bf16[256,896]{1,0:T(8,128)(2,1)}), bf16[4096,896]{1,0:T(8,128)(2,1)}) %all-gather.9.cloned.1.call-update) | async-done | bytes 7340048 | tf_op jit(solution)/shard_map/all_gather | solution.py:23
  155.6 79.3 %all-gather.11.cloned.1.call-done = bf16[896,4096]{1,0:T(8,128)(2,1)} async-done(((bf16[896,256]{1,0:T(8,128)(2,1)}), bf16[896,4096]{1,0:T(8,128)(2,1)}) %all-gather.11.cloned.1.call-update) | async-done | bytes 7340048 | tf_op jit(solution)/shard_map/all_gather | solution.py:49
  234.8 17.4 %fusion.2 = f32[512,4096]{1,0:T(8,128)} fusion(bf16[896,4096]{1,0:T(8,128)(2,1)} %all-gather.11.cloned.1.call-done, f32[512,896]{1,0:T(8,128)} %fusion.1, bf16[4096,896]{1,0:T(8,128)(2,1)} %all-gather.9.cloned.1.call-done, f32[4096]{0:T(1024)S(1)} %copy-done.1, f32[512]{0:T(512)S(1)} %add_rsqrt_fusion, bf16[512,4096]{1,0:T(8,128)(2,1)} %param.9), kind=kOutput, calls=%fused_computation.8 | convolution fusion | flops 7527333888 | bytes 29116416 | tf_op jit(solution)/shard_map/dot_general | solution.py:47
  252.2 9.8 %reshape.32 = f32[128,4,4096]{2,1,0:T(4,128)} reshape(f32[512,4096]{1,0:T(8,128)} %fusion.2) | data formatting | bytes 16777216 | tf_op jit(solution)/shard_map/reshape | solution.py:52
  262.0 10.0 %reduce_sum.76 = f32[128,4096]{1,0:T(8,128)} reduce(f32[128,4,4096]{2,1,0:T(4,128)} %reshape.32, f32[]{:T(128)} %constant.15.clone.1), dimensions={1}, to_apply=%region_4.5 | reduce | flops 1572864 | bytes 10485764 | tf_op jit(solution)/shard_map/reduce_sum | solution.py:52
  272.1 6.5 convert_element_type.23
  278.6 1.3 constant_dynamic-slice_fusion
  279.9 1.3 reshape.31
  281.2 1.8 reduce_sum.74
  283.1 29.9 %reduce-scatter.2.cloned.1.call-done = f32[128,512]{1,0:T(8,128)} async-done(((f32[128,4096]{1,0:T(8,128)}), f32[128,512]{1,0:T(8,128)}) %reduce-scatter.2.cloned.1.call-update) | async-done | bytes 262160 | tf_op jit(solution)/shard_map/reduce_scatter | solution.py:53
  313.0 2.4 fusion.4
  315.4 0.0 all-gather.13.cloned.1.call-start
  315.5 70.9 %all-reduce.2.cloned.1.call-done = f32[128,1024]{1,0:T(8,128)} async-done(((f32[128,1024]{1,0:T(8,128)}), f32[128,1024]{1,0:T(8,128)}) %all-reduce.2.cloned.1.call-update) | async-done | bytes 524304 | tf_op jit(solution)/shard_map/psum | solution.py:59
  386.3 1.2 multiply_reduce_fusion.2
  387.5 1.8 multiply_convert_fusion.8
  389.4 0.3 all-gather.15.cloned.1.call-start
  389.7 0.1 convert_reduce_fusion
  389.8 1.8 multiply_reduce_fusion.1
  391.6 0.1 fusion.6
  391.8 53.2 %all-gather.13.cloned.1.call-done = bf16[2048,1024]{1,0:T(8,128)(2,1)} async-done(((bf16[128,1024]{1,0:T(8,128)(2,1)}), bf16[2048,1024]{1,0:T(8,128)(2,1)}) %all-gather.13.cloned.1.call-update) | async-done | bytes 4194320 | tf_op jit(solution)/shard_map/all_gather | solution.py:61
  445.0 4.9 fusion.16
  449.8 8.8 %psum.15 = f32[256]{0:T(256)S(1)} all-reduce(f32[256]{0:T(256)S(1)} %get-tuple-element.7), channel_id=1, replica_groups=mesh['gen'=8,'user'=16,'cand'=2] {'cand'}, use_global_device_ids=true, to_apply=%region_9.10 | all-reduce | flops 256 | bytes 2048 | tf_op jit(solution)/shard_map/psum | solution.py:67
  458.6 3.3 fusion.17
  462.0 303.7 %all-gather.15.cloned.1.call-done = f32[262144]{0:T(1024)} async-done(((f32[2048]{0:T(1024)}), f32[262144]{0:T(1024)}) %all-gather.15.cloned.1.call-update) | async-done | bytes 1048592 | tf_op jit(solution)/shard_map/all_gather | solution.py:78
  765.6 1.4 reshape.34
  767.0 0.7 reduce_sum.79
  (19 shorter events, 0.3 us)
Async XLA Ops:
  6.5 383.2 %copy-start = (bf16[1024,1024]{1,0:T(8,128)(2,1)S(1)}, bf16[1024,1024]{1,0:T(8,128)(2,1)}, u32[]{:S(2)}) copy-start(bf16[1024,1024]{1,0:T(8,128)(2,1)} %param.16) | copy-start | bytes 6291460
  6.5 75.7 %copy-start.1 = (f32[4096]{0:T(1024)S(1)}, f32[4096]{0:T(1024)}, u32[]{:S(2)}) copy-start(f32[4096]{0:T(1024)} %param.10) | copy-start | bytes 49156
  6.5 75.7 %all-gather.7.cloned.1.call-start = ((), (), s32[]{:S(2)}) async-start(), calls=%async_computation.1 | async-start | bytes 7798784 | tf_op jit(solution)/shard_map/all_gather | solution.py:22
  7.3 148.3 %all-gather.9.cloned.1.call-start = ((), (), s32[]{:S(2)}) async-start(), calls=%async_computation.2 | async-start | bytes 7798784 | tf_op jit(solution)/shard_map/all_gather | solution.py:23
  8.0 226.8 %all-gather.11.cloned.1.call-start = ((), (), s32[]{:S(2)}) async-start(), calls=%async_computation.3 | async-start | bytes 7798784 | tf_op jit(solution)/shard_map/all_gather | solution.py:49
  8.7 304.2 %reduce-scatter.2.cloned.1.call-start = ((), (), s32[]{:S(2)}) async-start(), calls=%async_computation.4 | async-start | bytes 2359296 | tf_op jit(solution)/shard_map/reduce_scatter | solution.py:53
  272.1 114.3 %all-reduce.2.cloned.1.call-start = ((), (), s32[]{:S(2)}) async-start(), calls=%async_computation.5 | async-start | bytes 1048576 | tf_op jit(solution)/shard_map/psum | solution.py:59
  279.9 109.7 %copy-start.2 = (s32[256]{0:T(256)S(1)}, s32[256]{0:T(256)}, u32[]{:S(2)}) copy-start(s32[256]{0:T(256)} %param.17) | copy-start | bytes 3076
  315.4 129.5 %all-gather.13.cloned.1.call-start = ((), (), s32[]{:S(2)}) async-start(), calls=%async_computation.6 | async-start | bytes 4456448 | tf_op jit(solution)/shard_map/all_gather | solution.py:61
  389.4 376.3 %all-gather.15.cloned.1.call-start = ((), (), s32[]{:S(2)}) async-start(), calls=%async_computation.7 | async-start | bytes 1056768 | tf_op jit(solution)/shard_map/all_gather | solution.py:78
Sparse Core Ops, SparseCore 0:
  9.8 72.3 all-gather.6
  84.7 70.8 all-gather.8
  158.0 76.7 all-gather.10
  272.2 40.7 reduce-scatter.1
  315.5 70.7 all-reduce.1
  389.5 55.4 all-gather.12
  462.1 303.5 all-gather.14
